TPU v7x, 256 devices: a whole 4x4x8 slice. The times are simulated.
256 devices in a mesh: lat: 16 (over x, y_hi, core), lon: 16 (over y_lo, z).
Axes of the slice: x: 4, y: 4 (y_hi: 2, y_lo: 2; y = y_hi * 2 + y_lo), z: 8, core: 2. Of those that a mesh axis runs over, the one named last changes fastest.
Arguments:
- feature: bfloat16 [512, 512, 384], P('lat', 'lon'), may hold values from -6 to 6
- coverage: int32 [512, 512], P('lat', 'lon'), may hold values 0 or 1
- band_rows: int32 [16], replicated, may hold values from 3 to 32, as said below
- depth_weight: bfloat16 [7, 7, 384], replicated, may hold values from -0.875 to 0.875
- norm_gain: float32 [384], replicated, may hold values from 0.25 to 1.75
- norm_shift: float32 [384], replicated, may hold values from -3 to 3
- up_weight: bfloat16 [384, 1536], P('lon'), may hold values from -0.3125 to 0.3125
- up_bias: float32 [1536], replicated, may hold values from -3 to 3
- down_weight: bfloat16 [1536, 384], P('lon'), may hold values from -0.15625 to 0.15625
- down_bias: float32 [384], replicated, may hold values from -3 to 3
- layer_scale: float32 [384], replicated, may hold values from 0.3 to 1.5
- cotangent: bfloat16 [512, 512, 384], P('lat', 'lon'), may hold values from -6 to 6
Outputs:
- block_out: bfloat16 [512, 512, 384], P('lat', 'lon')
- grad_in: bfloat16 [512, 512, 384], P('lat', 'lon')
- grad_up: float32 [384, 1536], P('lon')
- grad_down: float32 [1536, 384], P('lon')
- grad_depth: float32 [7, 7, 384], replicated
Inputs may be any that keep to these rules, and one draw needn't show every extreme that they name: `band_rows`: every band has 3 or more rows, the bands' rows sum to 256, and one band has exactly 32.
All inputs are finite; a program needn't handle non-finite values. No bound on the sum of `coverage` on one device may be relied on, other than what follows from the above.
Results may differ from a plain program's by a relative error of at most 0.0066.
Values may be sent and summed in bfloat16 or wider, within the bound.
A program may use at most 64 MiB of HBM per device.

v0:
```python
import math
import jax
import jax.numpy as jnp
from jax import lax
from jax.sharding import PartitionSpec as P

BAND_MEAN = 16
SQRT_TWO_PI = 0.7978845608028654
CUBIC = 0.044715
EPSILON = 1e-06


def padded(array, sides, width):
    for axis, dim in sides:
        size, length = (lax.axis_size(axis), array.shape[dim])
        up = [(i, (i + 1) % size) for i in range(size)]
        down = [(j, i) for i, j in up]
        last = lax.slice_in_dim(array, length - width, length, axis=dim)
        initial = lax.slice_in_dim(array, 0, width, axis=dim)
        before = lax.ppermute(last, axis, up)
        after = lax.ppermute(initial, axis, down)
        array = jnp.concatenate([before, array, after], axis=dim)
    return array


def shifted(block, axis, distance):
    devices = range(lax.axis_size(axis))
    route = [(i - distance, i) for i in devices if i - distance in devices]
    return lax.ppermute(block, axis, route)


def smooth_gate(pre_act):
    argument = SQRT_TWO_PI * (pre_act + CUBIC * pre_act * pre_act * pre_act)
    return 0.5 * pre_act * (1.0 + jnp.tanh(argument))


def smooth_slope(pre_act):
    argument = SQRT_TWO_PI * (pre_act + CUBIC * pre_act * pre_act * pre_act)
    tangent = jnp.tanh(argument)
    return 0.5 * (1.0 + tangent) + 0.5 * pre_act * (1.0 - tangent * tangent) * SQRT_TWO_PI * (
        1.0 + 3.0 * CUBIC * pre_act * pre_act
    )


def extend(field, live_rows):
    widened = padded(field, (("lon", 1),), 3)
    last_rows = lax.dynamic_slice_in_dim(widened, live_rows - 3, 3, 0)
    from_above = shifted(last_rows, "lat", 1)
    from_below = shifted(widened[:3], "lat", -1)
    zero_rows = jnp.zeros((3,) + widened.shape[1:], widened.dtype)
    stacked = jnp.concatenate([from_above, widened, zero_rows], axis=0)
    return lax.dynamic_update_slice_in_dim(stacked, from_below, live_rows + 3, 0)


def shards(
    feature,
    coverage,
    band_rows,
    depth_weight,
    norm_gain,
    norm_shift,
    up_weight,
    up_bias,
    down_weight,
    down_bias,
    layer_scale,
    cotangent,
):
    rows_max, tile_cols, channels = feature.shape
    kernel = depth_weight.shape[0]
    live_rows = lax.dynamic_index_in_dim(band_rows, lax.axis_index("lat"), 0, keepdims=False)
    inside = jnp.arange(rows_max, dtype=jnp.int32) < live_rows
    covered = jnp.where(inside[:, None], coverage, 0).astype(jnp.bfloat16)
    masked = feature * covered[:, :, None]
    framed = extend(masked, live_rows)
    depth_out = jnp.zeros((rows_max, tile_cols, channels), jnp.float32)
    for row_off in range(kernel):
        for col_off in range(kernel):
            depth_out = depth_out + framed[
                row_off : row_off + rows_max, col_off : col_off + tile_cols
            ].astype(jnp.float32) * depth_weight[row_off, col_off].astype(jnp.float32)
    full_up, full_down = (
        lax.all_gather(up_weight, "lon", axis=0, tiled=True),
        lax.all_gather(down_weight, "lon", axis=0, tiled=True),
    )
    depth_rows = depth_out.reshape(-1, channels)
    center = jnp.mean(depth_rows, axis=-1, keepdims=True)
    offset = depth_rows - center
    scale_inv = lax.rsqrt(jnp.mean(offset * offset, axis=-1, keepdims=True) + EPSILON)
    standard = offset * scale_inv
    normed = (standard * norm_gain + norm_shift).astype(jnp.bfloat16)
    before = jnp.dot(normed, full_up, preferred_element_type=jnp.float32) + up_bias
    active = smooth_gate(before).astype(jnp.bfloat16)
    branch = jnp.dot(active, full_down, preferred_element_type=jnp.float32) + down_bias
    result = (feature.reshape(-1, channels).astype(jnp.float32) + layer_scale * branch).astype(
        jnp.bfloat16
    )
    cot_live = jnp.where(inside[:, None, None], cotangent, jnp.zeros_like(cotangent)).reshape(
        -1, channels
    )
    upstream = (layer_scale * cot_live.astype(jnp.float32)).astype(jnp.bfloat16)
    sum_down = lax.dot_general(
        active, upstream, (((0,), (0,)), ((), ())), preferred_element_type=jnp.float32
    )
    back_active = lax.dot_general(
        upstream, full_down, (((1,), (1,)), ((), ())), preferred_element_type=jnp.float32
    )
    back_before = (back_active * smooth_slope(before)).astype(jnp.bfloat16)
    sum_up = lax.dot_general(
        normed, back_before, (((0,), (0,)), ((), ())), preferred_element_type=jnp.float32
    )
    back_normed = lax.dot_general(
        back_before, full_up, (((1,), (1,)), ((), ())), preferred_element_type=jnp.float32
    )
    back_unit = back_normed * norm_gain
    back_depth = scale_inv * (
        back_unit
        - jnp.mean(back_unit, axis=-1, keepdims=True)
        - standard * jnp.mean(back_unit * standard, axis=-1, keepdims=True)
    )
    back_depth = back_depth.astype(jnp.bfloat16).reshape(rows_max, tile_cols, channels)
    framed_back = extend(back_depth, live_rows)
    spread = jnp.zeros((rows_max, tile_cols, channels), jnp.float32)
    tap_list = []
    for row_off in range(kernel):
        for col_off in range(kernel):
            spread = spread + framed_back[
                6 - row_off : 6 - row_off + rows_max, 6 - col_off : 6 - col_off + tile_cols
            ].astype(jnp.float32) * depth_weight[row_off, col_off].astype(jnp.float32)
            tap_list.append(
                jnp.sum(
                    framed[row_off : row_off + rows_max, col_off : col_off + tile_cols].astype(
                        jnp.float32
                    )
                    * back_depth.astype(jnp.float32),
                    axis=(0, 1),
                )
            )
    grad_local = (
        cotangent.astype(jnp.float32) + covered.astype(jnp.float32)[:, :, None] * spread
    ).astype(jnp.bfloat16)
    grad_in = jnp.where(inside[:, None, None], grad_local, jnp.zeros_like(grad_local))
    block_out = jnp.where(
        inside[:, None, None],
        result.reshape(rows_max, tile_cols, channels),
        jnp.zeros_like(feature),
    )
    rscale = 1.0 / math.sqrt(BAND_MEAN * lax.axis_size("lat") * tile_cols * lax.axis_size("lon"))
    tap_terms = jnp.stack(tap_list, axis=0).reshape(kernel, kernel, channels)
    grad_depth = lax.psum(tap_terms, ("lat", "lon")) * rscale
    up_part, down_part = (
        lax.psum_scatter(sum_up, "lon", scatter_dimension=0, tiled=True),
        lax.psum_scatter(sum_down, "lon", scatter_dimension=0, tiled=True),
    )
    up_part, down_part = lax.psum((up_part, down_part), "lat")
    return (block_out, grad_in, up_part * rscale, down_part * rscale, grad_depth)


def solution(mesh):
    placed = (
        P("lat", "lon", None),
        P("lat", "lon"),
        P(),
        P(),
        P(),
        P(),
        P("lon", None),
        P(),
        P("lon", None),
        P(),
        P(),
        P("lat", "lon", None),
    )
    return jax.shard_map(
        shards,
        mesh=mesh,
        in_specs=placed,
        out_specs=(
            P("lat", "lon", None),
            P("lat", "lon", None),
            P("lon", None),
            P("lon", None),
            P(),
        ),
        check_vma=False,
    )
```

profile of v0, /device:TPU:8, one launch (start us, length us, event | category | flops | bytes accessed | tf_op | source)
XLA Modules:
  0.0 711.5 jit_solution(1951065629706237876)
XLA Ops:
  7.2 0.0 all-gather.3.cloned.1.call-start
  7.2 0.7 all-gather.3.cloned.1.call-update
  7.9 0.0 all-gather.5.cloned.1.call-start
  8.0 1.2 dynamic_slice.10
  9.2 0.6 iota_compare_fusion
  9.9 0.8 fusion.108
  10.7 1.3 broadcast_multiply_fusion
  12.0 0.1 fusion.114
  12.1 2.0 collective-permute-start
  14.1 3.9 collective-permute-start.1
  18.0 0.0 all-gather.5.cloned.1.call-update
  18.0 0.0 all-reduce.4.cloned.1.call-start
  20.7 0.1 convert_reduce_fusion.47
  21.0 0.7 pad.12.clone
  21.7 0.1 convert_reduce_fusion.48
  22.0 0.6 pad_maximum_fusion
  22.6 1.5 collective-permute-start.2
  24.0 0.7 convert_reduce_fusion.46
  24.7 1.3 collective-permute-start.3
  26.0 1.1 maximum_maximum_fusion
  27.1 3.4 collective-permute-done.3
  30.9 12.5 %fusion.109 = (f32[32,32]{1,0:T(8,128)S(1)}, f32[32,32,384]{2,1,0:T(8,128)S(1)}) fusion(f32[384]{0:T(512)} %get-tuple-element.103, bf16[38,38,384]{2,1,0:T(8,128)(2,1)S(1)} %constant_dynamic-update-slice_fusion.1, f32[384]{0:T(512)} %get-tuple-element.104, f32[384]{0:T(512)S(1)} %get-tuple-element.57, f32[384]{0:T(512)S(1)} %get-tuple-element.58, ...), kind=kLoop, calls=%fused_computation.289 | loop fusion | flops 57801728 | bytes 40187392 | tf_op jit(solution)/shard_map/reduce_sum | solution.py:87
  43.5 0.1 div.15
  43.6 0.4 multiply_reduce_fusion.1
  44.0 0.1 rsqrt.12
  44.0 0.1 copy-done.87
  44.2 1.2 add_convert_fusion.1
  45.4 36.1 %all-gather.3.cloned.1.call-done = bf16[384,1536]{1,0:T(8,128)(2,1)} async-done(((bf16[24,1536]{1,0:T(8,128)(2,1)}), bf16[384,1536]{1,0:T(8,128)(2,1)}) %all-gather.3.cloned.1.call-update) | async-done | bytes 1179664 | tf_op jit(solution)/shard_map/all_gather | solution.py:83
  81.5 7.8 %multiply_convert_fusion = (bf16[1024,1536]{1,0:T(8,128)(2,1)}, f32[1024,1536]{1,0:T(8,128)}) fusion(f32[1536]{0:T(1024)} %param.19, bf16[1024,384]{1,0:T(8,128)(2,1)} %add_convert_fusion.1, bf16[384,1536]{1,0:T(8,128)(2,1)} %all-gather.3.cloned.1.call-done), kind=kOutput, calls=%fused_computation.58 | convolution fusion | flops 1223688192 | bytes 11409408 | tf_op jit(solution)/shard_map/dot_general | solution.py:92
  89.3 61.2 %all-gather.5.cloned.1.call-done = bf16[1536,384]{1,0:T(8,128)(2,1)} async-done(((bf16[96,384]{1,0:T(8,128)(2,1)}), bf16[1536,384]{1,0:T(8,128)(2,1)}) %all-gather.5.cloned.1.call-update) | async-done | bytes 1179664 | tf_op jit(solution)/shard_map/all_gather | solution.py:84
  150.5 4.2 fusion.105
  154.7 1.1 broadcast_select_fusion.1
  155.8 0.2 fusion.104
  156.1 1.2 copy-done.92
  157.3 5.4 fusion.6
  162.7 2.0 fusion.107
  164.8 5.0 fusion.103
  169.7 3.0 fusion.67
  172.8 4.0 fusion.85
  177.3 0.2 stack.199
  177.5 0.7 reshape.86
  178.2 0.0 reduce-scatter.5.cloned.1.call-start
  178.2 5.2 fusion.116
  183.4 0.0 reduce-scatter.3.cloned.1.call-start
  183.5 1.1 copy-done.5
  184.6 4.7 fusion.115
  189.3 0.0 all-reduce.6.cloned.1.call-start
  189.3 0.1 fusion.113
  189.4 0.7 collective-permute-start.4
  190.1 3.5 collective-permute-start.5
  193.6 2.6 collective-permute-done.4
  196.3 0.6 pad_maximum_fusion.1
  197.2 1.3 collective-permute-start.6
  198.5 218.1 %all-reduce.4.cloned.1.call-done = f32[7,7,384]{2,1,0:T(8,128)} async-done(((f32[7,7,384]{2,1,0:T(8,128)}), f32[7,7,384]{2,1,0:T(8,128)}) %all-reduce.4.cloned.1.call-update) | async-done | bytes 75280 | tf_op jit(solution)/shard_map/psum | solution.py:150
  416.6 1.5 broadcast_multiply_fusion.3
  418.1 1.3 collective-permute-start.7
  419.4 1.1 maximum_maximum_fusion.1
  420.5 0.8 collective-permute-done.7
  421.3 68.6 %reduce-scatter.5.cloned.1.call-done = f32[96,384]{1,0:T(8,128)} async-done(((f32[1536,384]{1,0:T(8,128)}), f32[96,384]{1,0:T(8,128)}) %reduce-scatter.5.cloned.1.call-update) | async-done | bytes 147472 | tf_op jit(solution)/shard_map/reduce_scatter | solution.py:153
  489.9 73.4 %reduce-scatter.3.cloned.1.call-done = f32[24,1536]{1,0:T(8,128)} async-done(((f32[384,1536]{1,0:T(8,128)}), f32[24,1536]{1,0:T(8,128)}) %reduce-scatter.3.cloned.1.call-update) | async-done | bytes 147472 | tf_op jit(solution)/shard_map/reduce_scatter | solution.py:152
  563.8 12.6 %broadcast_select_fusion = bf16[32,32,384]{2,1,0:T(8,128)(2,1)} fusion(pred[32]{0:T(512)(128)(4,1)} %copy-done.85, f32[384]{0:T(512)} %get-tuple-element.103, bf16[38,38,384]{2,1,0:T(8,128)(2,1)S(1)} %constant_dynamic-update-slice_fusion, f32[384]{0:T(512)} %get-tuple-element.104, f32[384]{0:T(512)S(1)} %copy-done.46, f32[384]{0:T(512)S(1)} %copy-done.48, ...), kind=kLoop, calls=%fused_computation.221 | loop fusion | flops 59375616 | bytes 40187424 | tf_op jit(solution)/shard_map/jit(_where)/select_n | solution.py:142
  576.3 125.2 %all-reduce.6.cloned.1.call-done = (f32[24,1536]{1,0:T(8,128)}, f32[96,384]{1,0:T(8,128)}) async-done(((f32[24,1536]{1,0:T(8,128)}, f32[96,384]{1,0:T(8,128)}), (f32[24,1536]{1,0:T(8,128)}, f32[96,384]{1,0:T(8,128)})) %all-reduce.6.cloned.1.call-update) | async-done | bytes 294928 | tf_op jit(solution)/shard_map/psum | solution.py:155
  701.5 1.6 broadcast_multiply_fusion.2
  703.1 1.6 broadcast_multiply_fusion.1
  (255 shorter events, 0.8 us)
Async XLA Ops:
  7.2 13.5 %copy-start.6 = (bf16[7,7,384]{2,1,0:T(8,128)(2,1)S(1)}, bf16[7,7,384]{2,1,0:T(8,128)(2,1)}, u32[]{:S(2)}) copy-start(bf16[7,7,384]{2,1,0:T(8,128)(2,1)} %param.15) | copy-start | bytes 112900
  7.2 74.3 %all-gather.3.cloned.1.call-start = ((), (), s32[]{:S(2)}) async-start(), calls=%async_computation.2 | async-start | bytes 1253376 | tf_op jit(solution)/shard_map/all_gather | solution.py:83
  7.9 142.6 %all-gather.5.cloned.1.call-start = ((), (), s32[]{:S(2)}) async-start(), calls=%async_computation.3 | async-start | bytes 1253376 | tf_op jit(solution)/shard_map/all_gather | solution.py:84
  12.1 9.8 %collective-permute-start = (bf16[32,3,384]{2,1,0:T(4,128)(2,1)S(1)}, bf16[32,3,384]{2,1,0:T(4,128)(2,1)S(1)}, u32[]{:S(2)}, u32[]{:S(2)}) collective-permute-start(bf16[32,3,384]{2,1,0:T(4,128)(2,1)S(1)} %get-tuple-element.118), channel_id=1, source_target_pairs={{0,1},{1,2},{2,3},{3,4},{4,5},{5,6},{6,7},{7,8},{8,9},{9,10},{10,1... | collective-permute-start | bytes 221192 | tf_op jit(solution)/shard_map/ppermute | solution.py:20
  14.1 7.9 %collective-permute-start.1 = (bf16[32,3,384]{2,1,0:T(4,128)(2,1)S(1)}, bf16[32,3,384]{2,1,0:T(4,128)(2,1)S(1)}, u32[]{:S(2)}, u32[]{:S(2)}) collective-permute-start(bf16[32,3,384]{2,1,0:T(4,128)(2,1)S(1)} %get-tuple-element.119), channel_id=1, source_target_pairs={{1,0},{2,1},{3,2},{4,3},{5,4},{6,5},{7,6},{8,7},{9,8},{10,9},{11,1... | collective-permute-start | bytes 221192 | tf_op jit(solution)/shard_map/ppermute | solution.py:21
  18.0 398.6 %all-reduce.4.cloned.1.call-start = ((), (), s32[]{:S(2)}) async-start(), calls=%async_computation.6 | async-start | bytes 172032 | tf_op jit(solution)/shard_map/psum | solution.py:150
  20.8 9.8 %copy-start.9 = (f32[384]{0:T(512)}, f32[384]{0:T(512)S(1)}, u32[]{:S(2)}) copy-start(f32[384]{0:T(512)S(1)} %get-tuple-element.77) | copy-start | bytes 4612
  20.8 9.8 %copy-start.11 = (f32[384]{0:T(512)}, f32[384]{0:T(512)S(1)}, u32[]{:S(2)}) copy-start(f32[384]{0:T(512)S(1)} %get-tuple-element.78) | copy-start | bytes 4612
  20.8 9.8 %copy-start.13 = (f32[384]{0:T(512)}, f32[384]{0:T(512)S(1)}, u32[]{:S(2)}) copy-start(f32[384]{0:T(512)S(1)} %get-tuple-element.79) | copy-start | bytes 4612
  20.8 9.8 %copy-start.15 = (f32[384]{0:T(512)}, f32[384]{0:T(512)S(1)}, u32[]{:S(2)}) copy-start(f32[384]{0:T(512)S(1)} %get-tuple-element.80) | copy-start | bytes 4612
  20.8 9.8 %copy-start.17 = (f32[384]{0:T(512)}, f32[384]{0:T(512)S(1)}, u32[]{:S(2)}) copy-start(f32[384]{0:T(512)S(1)} %get-tuple-element.81) | copy-start | bytes 4612
  20.8 9.8 %copy-start.19 = (f32[384]{0:T(512)}, f32[384]{0:T(512)S(1)}, u32[]{:S(2)}) copy-start(f32[384]{0:T(512)S(1)} %get-tuple-element.82) | copy-start | bytes 4612
  22.6 3.4 collective-permute-start.2
  24.7 18.8 %copy-start.81 = (f32[384]{0:T(512)}, f32[384]{0:T(512)S(1)}, u32[]{:S(2)}) copy-start(f32[384]{0:T(512)S(1)} %get-tuple-element.94) | copy-start | bytes 4612
  24.7 18.8 %copy-start.83 = (f32[384]{0:T(512)}, f32[384]{0:T(512)S(1)}, u32[]{:S(2)}) copy-start(f32[384]{0:T(512)S(1)} %get-tuple-element.95) | copy-start | bytes 4612
  24.7 5.8 collective-permute-start.3
  45.4 105.1 %copy-start.2 = (bf16[32,32,384]{2,1,0:T(8,128)(2,1)S(1)}, bf16[32,32,384]{2,1,0:T(8,128)(2,1)}, u32[]{:S(2)}) copy-start(bf16[32,32,384]{2,1,0:T(8,128)(2,1)} %param.12) | copy-start | bytes 2359300
  178.2 311.8 %reduce-scatter.5.cloned.1.call-start = ((), (), s32[]{:S(2)}) async-start(), calls=%async_computation.5 | async-start | bytes 2506752 | tf_op jit(solution)/shard_map/reduce_scatter | solution.py:153
  183.4 379.9 %reduce-scatter.3.cloned.1.call-start = ((), (), s32[]{:S(2)}) async-start(), calls=%async_computation.4 | async-start | bytes 2506752 | tf_op jit(solution)/shard_map/reduce_scatter | solution.py:152
  189.3 512.2 %all-reduce.6.cloned.1.call-start = ((), (), s32[]{:S(2)}) async-start(), calls=%async_computation.7 | async-start | bytes 589824 | tf_op jit(solution)/shard_map/psum | solution.py:155
  189.4 6.8 collective-permute-start.4
  190.1 6.1 collective-permute-start.5
  196.8 366.5 %copy-start.1 = (bf16[32,32,384]{2,1,0:T(8,128)(2,1)S(1)}, bf16[32,32,384]{2,1,0:T(8,128)(2,1)}, u32[]{:S(2)}) copy-start(bf16[32,32,384]{2,1,0:T(8,128)(2,1)} %param.23) | copy-start | bytes 2359300
  196.8 366.5 %copy-start.8 = (f32[384]{0:T(512)S(1)}, f32[384]{0:T(512)}, u32[]{:S(2)}) copy-start(f32[384]{0:T(512)} %copy-done.7) | copy-start | bytes 4612
  196.8 366.5 %copy-start.10 = (f32[384]{0:T(512)S(1)}, f32[384]{0:T(512)}, u32[]{:S(2)}) copy-start(f32[384]{0:T(512)} %copy-done.9) | copy-start | bytes 4612
  196.8 366.5 %copy-start.12 = (f32[384]{0:T(512)S(1)}, f32[384]{0:T(512)}, u32[]{:S(2)}) copy-start(f32[384]{0:T(512)} %copy-done.11) | copy-start | bytes 4612
  196.9 366.5 %copy-start.14 = (f32[384]{0:T(512)S(1)}, f32[384]{0:T(512)}, u32[]{:S(2)}) copy-start(f32[384]{0:T(512)} %copy-done.13) | copy-start | bytes 4612
  196.9 366.5 %copy-start.16 = (f32[384]{0:T(512)S(1)}, f32[384]{0:T(512)}, u32[]{:S(2)}) copy-start(f32[384]{0:T(512)} %copy-done.15) | copy-start | bytes 4612
  196.9 366.5 %copy-start.18 = (f32[384]{0:T(512)S(1)}, f32[384]{0:T(512)}, u32[]{:S(2)}) copy-start(f32[384]{0:T(512)} %copy-done.17) | copy-start | bytes 4612
  196.9 366.5 %copy-start.20 = (f32[384]{0:T(512)S(1)}, f32[384]{0:T(512)}, u32[]{:S(2)}) copy-start(f32[384]{0:T(512)} %copy-done.19) | copy-start | bytes 4612
  196.9 366.5 %copy-start.22 = (f32[384]{0:T(512)S(1)}, f32[384]{0:T(512)}, u32[]{:S(2)}) copy-start(f32[384]{0:T(512)} %copy-done.21) | copy-start | bytes 4612
  196.9 366.5 %copy-start.24 = (f32[384]{0:T(512)S(1)}, f32[384]{0:T(512)}, u32[]{:S(2)}) copy-start(f32[384]{0:T(512)} %copy-done.23) | copy-start | bytes 4612
  196.9 366.5 %copy-start.26 = (f32[384]{0:T(512)S(1)}, f32[384]{0:T(512)}, u32[]{:S(2)}) copy-start(f32[384]{0:T(512)} %copy-done.25) | copy-start | bytes 4612
  196.9 366.5 %copy-start.28 = (f32[384]{0:T(512)S(1)}, f32[384]{0:T(512)}, u32[]{:S(2)}) copy-start(f32[384]{0:T(512)} %copy-done.27) | copy-start | bytes 4612
  196.9 366.5 %copy-start.30 = (f32[384]{0:T(512)S(1)}, f32[384]{0:T(512)}, u32[]{:S(2)}) copy-start(f32[384]{0:T(512)} %copy-done.29) | copy-start | bytes 4612
  196.9 366.5 %copy-start.32 = (f32[384]{0:T(512)S(1)}, f32[384]{0:T(512)}, u32[]{:S(2)}) copy-start(f32[384]{0:T(512)} %copy-done.31) | copy-start | bytes 4612
  197.0 366.5 %copy-start.34 = (f32[384]{0:T(512)S(1)}, f32[384]{0:T(512)}, u32[]{:S(2)}) copy-start(f32[384]{0:T(512)} %copy-done.33) | copy-start | bytes 4612
  197.0 366.5 %copy-start.36 = (f32[384]{0:T(512)S(1)}, f32[384]{0:T(512)}, u32[]{:S(2)}) copy-start(f32[384]{0:T(512)} %copy-done.35) | copy-start | bytes 4612
  197.0 366.5 %copy-start.38 = (f32[384]{0:T(512)S(1)}, f32[384]{0:T(512)}, u32[]{:S(2)}) copy-start(f32[384]{0:T(512)} %copy-done.37) | copy-start | bytes 4612
  197.0 366.5 %copy-start.40 = (f32[384]{0:T(512)S(1)}, f32[384]{0:T(512)}, u32[]{:S(2)}) copy-start(f32[384]{0:T(512)} %copy-done.39) | copy-start | bytes 4612
  197.0 366.5 %copy-start.42 = (f32[384]{0:T(512)S(1)}, f32[384]{0:T(512)}, u32[]{:S(2)}) copy-start(f32[384]{0:T(512)} %copy-done.41) | copy-start | bytes 4612
  197.0 366.5 %copy-start.44 = (f32[384]{0:T(512)S(1)}, f32[384]{0:T(512)}, u32[]{:S(2)}) copy-start(f32[384]{0:T(512)} %copy-done.43) | copy-start | bytes 4612
  197.0 366.5 %copy-start.46 = (f32[384]{0:T(512)S(1)}, f32[384]{0:T(512)}, u32[]{:S(2)}) copy-start(f32[384]{0:T(512)} %copy-done.45) | copy-start | bytes 4612
  197.0 366.5 %copy-start.48 = (f32[384]{0:T(512)S(1)}, f32[384]{0:T(512)}, u32[]{:S(2)}) copy-start(f32[384]{0:T(512)} %copy-done.47) | copy-start | bytes 4612
  197.0 366.5 %copy-start.50 = (f32[384]{0:T(512)S(1)}, f32[384]{0:T(512)}, u32[]{:S(2)}) copy-start(f32[384]{0:T(512)} %copy-done.49) | copy-start | bytes 4612
  197.0 366.5 %copy-start.52 = (f32[384]{0:T(512)S(1)}, f32[384]{0:T(512)}, u32[]{:S(2)}) copy-start(f32[384]{0:T(512)} %copy-done.51) | copy-start | bytes 4612
  197.1 366.5 %copy-start.54 = (f32[384]{0:T(512)S(1)}, f32[384]{0:T(512)}, u32[]{:S(2)}) copy-start(f32[384]{0:T(512)} %copy-done.53) | copy-start | bytes 4612
  197.1 366.5 %copy-start.56 = (f32[384]{0:T(512)S(1)}, f32[384]{0:T(512)}, u32[]{:S(2)}) copy-start(f32[384]{0:T(512)} %copy-done.55) | copy-start | bytes 4612
  197.1 366.5 %copy-start.58 = (f32[384]{0:T(512)S(1)}, f32[384]{0:T(512)}, u32[]{:S(2)}) copy-start(f32[384]{0:T(512)} %copy-done.57) | copy-start | bytes 4612
  197.1 366.5 %copy-start.60 = (f32[384]{0:T(512)S(1)}, f32[384]{0:T(512)}, u32[]{:S(2)}) copy-start(f32[384]{0:T(512)} %copy-done.59) | copy-start | bytes 4612
  197.1 366.5 %copy-start.62 = (f32[384]{0:T(512)S(1)}, f32[384]{0:T(512)}, u32[]{:S(2)}) copy-start(f32[384]{0:T(512)} %copy-done.61) | copy-start | bytes 4612
  197.1 366.5 %copy-start.64 = (f32[384]{0:T(512)S(1)}, f32[384]{0:T(512)}, u32[]{:S(2)}) copy-start(f32[384]{0:T(512)} %copy-done.63) | copy-start | bytes 4612
  197.1 366.5 %copy-start.66 = (f32[384]{0:T(512)S(1)}, f32[384]{0:T(512)}, u32[]{:S(2)}) copy-start(f32[384]{0:T(512)} %copy-done.65) | copy-start | bytes 4612
  197.1 366.5 %copy-start.68 = (f32[384]{0:T(512)S(1)}, f32[384]{0:T(512)}, u32[]{:S(2)}) copy-start(f32[384]{0:T(512)} %copy-done.67) | copy-start | bytes 4612
  197.1 366.5 %copy-start.70 = (f32[384]{0:T(512)S(1)}, f32[384]{0:T(512)}, u32[]{:S(2)}) copy-start(f32[384]{0:T(512)} %copy-done.69) | copy-start | bytes 4612
  197.1 366.5 %copy-start.72 = (f32[384]{0:T(512)S(1)}, f32[384]{0:T(512)}, u32[]{:S(2)}) copy-start(f32[384]{0:T(512)} %copy-done.71) | copy-start | bytes 4612
  197.2 366.5 %copy-start.74 = (f32[384]{0:T(512)S(1)}, f32[384]{0:T(512)}, u32[]{:S(2)}) copy-start(f32[384]{0:T(512)} %copy-done.73) | copy-start | bytes 4612
  197.2 366.5 %copy-start.76 = (f32[384]{0:T(512)S(1)}, f32[384]{0:T(512)}, u32[]{:S(2)}) copy-start(f32[384]{0:T(512)} %copy-done.75) | copy-start | bytes 4612
  197.2 366.5 %copy-start.78 = (f32[384]{0:T(512)S(1)}, f32[384]{0:T(512)}, u32[]{:S(2)}) copy-start(f32[384]{0:T(512)} %copy-done.77) | copy-start | bytes 4612
  197.2 366.5 %copy-start.80 = (f32[384]{0:T(512)S(1)}, f32[384]{0:T(512)}, u32[]{:S(2)}) copy-start(f32[384]{0:T(512)} %copy-done.79) | copy-start | bytes 4612
  197.2 366.5 %copy-start.82 = (f32[384]{0:T(512)S(1)}, f32[384]{0:T(512)}, u32[]{:S(2)}) copy-start(f32[384]{0:T(512)} %copy-done.81) | copy-start | bytes 4612
  197.2 366.5 %copy-start.84 = (f32[384]{0:T(512)S(1)}, f32[384]{0:T(512)}, u32[]{:S(2)}) copy-start(f32[384]{0:T(512)} %copy-done.83) | copy-start | bytes 4612
  197.2 222.2 %collective-permute-start.6 = (bf16[3,38,384]{2,1,0:T(8,128)(2,1)S(1)}, bf16[3,38,384]{2,1,0:T(8,128)(2,1)S(1)}, u32[]{:S(2)}, u32[]{:S(2)}) collective-permute-start(bf16[3,38,384]{2,1,0:T(8,128)(2,1)S(1)} %get-tuple-element.113), channel_id=1, source_target_pairs={{0,16},{16,32},{32,48},{48,64},{64,80},{80,96},{96,112},{112,128},... | collective-permute-start | bytes 262664 | tf_op jit(solution)/shard_map/ppermute | solution.py:29
  418.1 3.2 collective-permute-start.7
  (46 other events, 333.8 us)
Sparse Core Ops, SparseCore 0:
  9.8 71.6 all-gather.2
  83.3 67.1 all-gather.4
  178.3 238.2 all-reduce.3
  419.0 70.8 reduce-scatter.4
  492.3 70.9 reduce-scatter.2
  565.9 135.5 all-reduce.5
where the time goes:
time: 712 us
  waiting for transfers between devices  590 us (83%)
  other arithmetic  51.7 us (7%)
  matrix products  29.3 us (4%)
  between operations  18.7 us (3%)
  starting transfers between devices  15.7 us (2%)
    psum x1, waiting for transfers between devices, shards(): grad_depth = lax.psum(tap_terms, ('lat', 'lon')) * rscale  218 us
    psum x1, waiting for transfers between devices, shards(): up_part, down_part = lax.psum((up_part, down_part), 'lat')  125 us
    reduce_scatter x1, waiting for transfers between devices, shards(): lax.psum_scatter(sum_up, 'lon', scatter_dimension=0, tiled=True)  73.4 us
    reduce_scatter x1, waiting for transfers between devices, shards(): lax.psum_scatter(sum_down, 'lon', scatter_dimension=0, tiled=True)  68.6 us
    all_gather x1, waiting for transfers between devices, shards(): lax.all_gather(down_weight, 'lon', axis=0, tiled=True)  61.2 us
    all_gather x1, waiting for transfers between devices, shards(): lax.all_gather(up_weight, 'lon', axis=0, tiled=True)  36.1 us
  transfers between devices with their start and end apart: 14, of which 9 were waited for; matrix products, arithmetic and copies ran while one was open for 8% of the time, Pallas kernels for 0%

commit v1 on v0

--- a/solution.py
+++ b/solution.py
@@ -1,3 +1,4 @@
+import functools
 import math
 import jax
 import jax.numpy as jnp
@@ -8,6 +9,15 @@
 SQRT_TWO_PI = 0.7978845608028654
 CUBIC = 0.044715
 EPSILON = 1e-06
+
+
+def derive_frames(local_values, group_axis, axis_key):
+    for ii in (group_axis, axis_key):
+        local_values = jax.lax.psum(local_values, ii)
+    return local_values
+
+
+_map_frame = functools.partial(derive_frames, group_axis="lon", axis_key="lat")
 
 
 def padded(array, sides, width):
@@ -147,7 +157,7 @@
     )
     rscale = 1.0 / math.sqrt(BAND_MEAN * lax.axis_size("lat") * tile_cols * lax.axis_size("lon"))
     tap_terms = jnp.stack(tap_list, axis=0).reshape(kernel, kernel, channels)
-    grad_depth = lax.psum(tap_terms, ("lat", "lon")) * rscale
+    grad_depth = _map_frame(tap_terms) * rscale
     up_part, down_part = (
         lax.psum_scatter(sum_up, "lon", scatter_dimension=0, tiled=True),
         lax.psum_scatter(sum_down, "lon", scatter_dimension=0, tiled=True),

time: 712 us -> 611 us (0.86)
  waiting for transfers between devices: 590 us -> 487 us
    psum x1, waiting for transfers between devices: 218 us -> 99.9 us  [derive_frames(): local_values = jax.lax.psum(local_values, ii)]
    reduce_scatter x1, waiting for transfers between devices: 68.6 us -> 76.2 us  [shards(): lax.psum_scatter(sum_down, 'lon', scatter_dimension=0, tiled=True)]
  transfers between devices with their start and end apart: 14 -> 14, of which waited for: 9 -> 9; matrix products, arithmetic and copies ran while one was open for 8% -> 9% of each run, Pallas kernels for 0% -> 0%
where the time goes in v1:
time: 611 us; the launch traced here: 609 us
  waiting for transfers between devices  487 us (80%)
  other arithmetic  51.7 us (8%)
  matrix products  29.3 us (5%)
  between operations  18.7 us (3%)
  starting transfers between devices  15.7 us (3%)
    psum x1, waiting for transfers between devices, shards(): up_part, down_part = lax.psum((up_part, down_part), 'lat')  130 us
    psum x1, waiting for transfers between devices, derive_frames(): local_values = jax.lax.psum(local_values, ii)  99.9 us
    reduce_scatter x1, waiting for transfers between devices, shards(): lax.psum_scatter(sum_down, 'lon', scatter_dimension=0, tiled=True)  76.2 us
    reduce_scatter x1, waiting for transfers between devices, shards(): lax.psum_scatter(sum_up, 'lon', scatter_dimension=0, tiled=True)  73.6 us
    all_gather x1, waiting for transfers between devices, shards(): lax.all_gather(down_weight, 'lon', axis=0, tiled=True)  61.2 us
    all_gather x1, waiting for transfers between devices, shards(): lax.all_gather(up_weight, 'lon', axis=0, tiled=True)  36.1 us
    select_n x1, other arithmetic, shards(): jnp.where(inside[:, None, None], grad_local, jnp.zeros_like(grad_local))  12.6 us
    reduce_sum x1, other arithmetic, shards(): center = jnp.mean(depth_rows, axis=-1, keepdims=True)  12.5 us
  transfers between devices with their start and end apart: 14, of which 9 were waited for; matrix products, arithmetic and copies ran while one was open for 9% of the time, Pallas kernels for 0%

profile of v1, /device:TPU:8, one launch (start us, length us, event | category | flops | bytes accessed | tf_op | source)
XLA Modules:
  0.0 608.8 jit_solution(8314623124003333438)
XLA Ops:
  7.2 0.0 all-gather.3.cloned.1.call-start
  7.2 0.7 all-gather.3.cloned.1.call-update
  7.9 0.0 all-gather.5.cloned.1.call-start
  8.0 1.2 dynamic_slice.10
  9.2 0.6 iota_compare_fusion
  9.9 0.8 fusion.108
  10.7 1.3 broadcast_multiply_fusion
  12.0 0.1 fusion.114
  12.1 2.0 collective-permute-start
  14.1 3.9 collective-permute-start.1
  18.0 0.0 all-gather.5.cloned.1.call-update
  18.0 0.0 all-reduce.4.cloned.1.call-start
  20.7 0.1 convert_reduce_fusion.47
  21.0 0.7 pad.12.clone
  21.7 0.1 convert_reduce_fusion.48
  22.0 0.6 pad_maximum_fusion
  22.6 1.5 collective-permute-start.2
  24.0 0.7 convert_reduce_fusion.46
  24.7 1.3 collective-permute-start.3
  26.0 1.1 maximum_maximum_fusion
  27.1 3.4 collective-permute-done.3
  30.9 12.5 %fusion.109 = (f32[32,32]{1,0:T(8,128)S(1)}, f32[32,32,384]{2,1,0:T(8,128)S(1)}) fusion(f32[384]{0:T(512)} %get-tuple-element.103, bf16[38,38,384]{2,1,0:T(8,128)(2,1)S(1)} %constant_dynamic-update-slice_fusion.1, f32[384]{0:T(512)} %get-tuple-element.104, f32[384]{0:T(512)S(1)} %get-tuple-element.57, f32[384]{0:T(512)S(1)} %get-tuple-element.58, ...), kind=kLoop, calls=%fused_computation.289 | loop fusion | flops 57801728 | bytes 40187392 | tf_op jit(solution)/shard_map/reduce_sum | solution.py:97
  43.5 0.1 div.15
  43.6 0.4 multiply_reduce_fusion.1
  44.0 0.1 rsqrt.12
  44.0 0.1 copy-done.87
  44.2 1.2 add_convert_fusion.1
  45.4 36.1 %all-gather.3.cloned.1.call-done = bf16[384,1536]{1,0:T(8,128)(2,1)} async-done(((bf16[24,1536]{1,0:T(8,128)(2,1)}), bf16[384,1536]{1,0:T(8,128)(2,1)}) %all-gather.3.cloned.1.call-update) | async-done | bytes 1179664 | tf_op jit(solution)/shard_map/all_gather | solution.py:93
  81.5 7.8 %multiply_convert_fusion = (bf16[1024,1536]{1,0:T(8,128)(2,1)}, f32[1024,1536]{1,0:T(8,128)}) fusion(f32[1536]{0:T(1024)} %param.19, bf16[1024,384]{1,0:T(8,128)(2,1)} %add_convert_fusion.1, bf16[384,1536]{1,0:T(8,128)(2,1)} %all-gather.3.cloned.1.call-done), kind=kOutput, calls=%fused_computation.58 | convolution fusion | flops 1223688192 | bytes 11409408 | tf_op jit(solution)/shard_map/dot_general | solution.py:102
  89.3 61.2 %all-gather.5.cloned.1.call-done = bf16[1536,384]{1,0:T(8,128)(2,1)} async-done(((bf16[96,384]{1,0:T(8,128)(2,1)}), bf16[1536,384]{1,0:T(8,128)(2,1)}) %all-gather.5.cloned.1.call-update) | async-done | bytes 1179664 | tf_op jit(solution)/shard_map/all_gather | solution.py:94
  150.5 4.2 fusion.105
  154.7 1.1 broadcast_select_fusion.1
  155.8 0.2 fusion.104
  156.1 1.2 copy-done.92
  157.3 5.4 fusion.6
  162.7 2.0 fusion.107
  164.8 5.0 fusion.103
  169.7 3.0 fusion.67
  172.8 4.0 fusion.85
  177.3 0.2 stack.199
  177.5 0.7 reshape.86
  178.2 0.0 reduce-scatter.5.cloned.1.call-start
  178.2 5.2 fusion.116
  183.4 0.0 reduce-scatter.3.cloned.1.call-start
  183.5 1.1 copy-done.5
  184.6 4.7 fusion.115
  189.3 0.0 all-reduce.6.cloned.1.call-start
  189.3 0.1 fusion.113
  189.4 0.7 collective-permute-start.4
  190.1 3.5 collective-permute-start.5
  193.6 2.6 collective-permute-done.4
  196.3 0.6 pad_maximum_fusion.1
  197.2 1.3 collective-permute-start.6
  198.5 1.3 collective-permute-start.7
  199.9 1.1 maximum_maximum_fusion.1
  201.0 3.3 collective-permute-done.7
  204.3 99.9 %all-reduce.4.cloned.1.call-done = f32[7,7,384]{2,1,0:T(8,128)} async-done(((f32[7,7,384]{2,1,0:T(8,128)}), f32[7,7,384]{2,1,0:T(8,128)}) %all-reduce.4.cloned.1.call-update) | async-done | bytes 75280 | tf_op jit(solution)/shard_map/psum | solution.py:16
  304.2 76.2 %reduce-scatter.5.cloned.1.call-done = f32[96,384]{1,0:T(8,128)} async-done(((f32[1536,384]{1,0:T(8,128)}), f32[96,384]{1,0:T(8,128)}) %reduce-scatter.5.cloned.1.call-update) | async-done | bytes 147472 | tf_op jit(solution)/shard_map/reduce_scatter | solution.py:163
  380.4 73.6 %reduce-scatter.3.cloned.1.call-done = f32[24,1536]{1,0:T(8,128)} async-done(((f32[384,1536]{1,0:T(8,128)}), f32[24,1536]{1,0:T(8,128)}) %reduce-scatter.3.cloned.1.call-update) | async-done | bytes 147472 | tf_op jit(solution)/shard_map/reduce_scatter | solution.py:162
  454.4 12.6 %broadcast_select_fusion = bf16[32,32,384]{2,1,0:T(8,128)(2,1)} fusion(pred[32]{0:T(512)(128)(4,1)} %copy-done.85, f32[384]{0:T(512)} %get-tuple-element.103, bf16[38,38,384]{2,1,0:T(8,128)(2,1)S(1)} %constant_dynamic-update-slice_fusion, f32[384]{0:T(512)} %get-tuple-element.104, f32[384]{0:T(512)S(1)} %copy-done.46, f32[384]{0:T(512)S(1)} %copy-done.48, ...), kind=kLoop, calls=%fused_computation.221 | loop fusion | flops 59375616 | bytes 40187424 | tf_op jit(solution)/shard_map/jit(_where)/select_n | solution.py:152
  467.0 130.2 %all-reduce.6.cloned.1.call-done = (f32[24,1536]{1,0:T(8,128)}, f32[96,384]{1,0:T(8,128)}, f32[7,7,384]{2,1,0:T(8,128)}) async-done(((f32[24,1536]{1,0:T(8,128)}, f32[96,384]{1,0:T(8,128)}, f32[7,7,384]{2,1,0:T(8,128)}), (f32[24,1536]{1,0:T(8,128)}, f32[96,384]{1,0:T(8,128)}, f32[7,7,384]{2,1,0:T(8,128)})) %all-reduce.6.cloned.1.call-update) | async-done | bytes 370192 | tf_op jit(solution)/shard_map/psum | solution.py:165
  597.3 1.6 broadcast_multiply_fusion.2
  598.8 1.5 broadcast_multiply_fusion.3
  600.4 1.6 broadcast_multiply_fusion.1
  (255 shorter events, 0.8 us)
Async XLA Ops:
  7.2 13.5 %copy-start.6 = (bf16[7,7,384]{2,1,0:T(8,128)(2,1)S(1)}, bf16[7,7,384]{2,1,0:T(8,128)(2,1)}, u32[]{:S(2)}) copy-start(bf16[7,7,384]{2,1,0:T(8,128)(2,1)} %param.15) | copy-start | bytes 112900
  7.2 74.3 %all-gather.3.cloned.1.call-start = ((), (), s32[]{:S(2)}) async-start(), calls=%async_computation.2 | async-start | bytes 1253376 | tf_op jit(solution)/shard_map/all_gather | solution.py:93
  7.9 142.6 %all-gather.5.cloned.1.call-start = ((), (), s32[]{:S(2)}) async-start(), calls=%async_computation.3 | async-start | bytes 1253376 | tf_op jit(solution)/shard_map/all_gather | solution.py:94
  12.1 9.8 %collective-permute-start = (bf16[32,3,384]{2,1,0:T(4,128)(2,1)S(1)}, bf16[32,3,384]{2,1,0:T(4,128)(2,1)S(1)}, u32[]{:S(2)}, u32[]{:S(2)}) collective-permute-start(bf16[32,3,384]{2,1,0:T(4,128)(2,1)S(1)} %get-tuple-element.119), channel_id=1, source_target_pairs={{0,1},{1,2},{2,3},{3,4},{4,5},{5,6},{6,7},{7,8},{8,9},{9,10},{10,1... | collective-permute-start | bytes 221192 | tf_op jit(solution)/shard_map/ppermute | solution.py:30
  14.1 7.9 %collective-permute-start.1 = (bf16[32,3,384]{2,1,0:T(4,128)(2,1)S(1)}, bf16[32,3,384]{2,1,0:T(4,128)(2,1)S(1)}, u32[]{:S(2)}, u32[]{:S(2)}) collective-permute-start(bf16[32,3,384]{2,1,0:T(4,128)(2,1)S(1)} %get-tuple-element.120), channel_id=1, source_target_pairs={{1,0},{2,1},{3,2},{4,3},{5,4},{6,5},{7,6},{8,7},{9,8},{10,9},{11,1... | collective-permute-start | bytes 221192 | tf_op jit(solution)/shard_map/ppermute | solution.py:31
  18.0 286.2 %all-reduce.4.cloned.1.call-start = ((), (), s32[]{:S(2)}) async-start(), calls=%async_computation.6 | async-start | bytes 172032 | tf_op jit(solution)/shard_map/psum | solution.py:16
  20.8 9.8 %copy-start.9 = (f32[384]{0:T(512)}, f32[384]{0:T(512)S(1)}, u32[]{:S(2)}) copy-start(f32[384]{0:T(512)S(1)} %get-tuple-element.77) | copy-start | bytes 4612
  20.8 9.8 %copy-start.11 = (f32[384]{0:T(512)}, f32[384]{0:T(512)S(1)}, u32[]{:S(2)}) copy-start(f32[384]{0:T(512)S(1)} %get-tuple-element.78) | copy-start | bytes 4612
  20.8 9.8 %copy-start.13 = (f32[384]{0:T(512)}, f32[384]{0:T(512)S(1)}, u32[]{:S(2)}) copy-start(f32[384]{0:T(512)S(1)} %get-tuple-element.79) | copy-start | bytes 4612
  20.8 9.8 %copy-start.15 = (f32[384]{0:T(512)}, f32[384]{0:T(512)S(1)}, u32[]{:S(2)}) copy-start(f32[384]{0:T(512)S(1)} %get-tuple-element.80) | copy-start | bytes 4612
  20.8 9.8 %copy-start.17 = (f32[384]{0:T(512)}, f32[384]{0:T(512)S(1)}, u32[]{:S(2)}) copy-start(f32[384]{0:T(512)S(1)} %get-tuple-element.81) | copy-start | bytes 4612
  20.8 9.8 %copy-start.19 = (f32[384]{0:T(512)}, f32[384]{0:T(512)S(1)}, u32[]{:S(2)}) copy-start(f32[384]{0:T(512)S(1)} %get-tuple-element.82) | copy-start | bytes 4612
  22.6 3.4 collective-permute-start.2
  24.7 18.8 %copy-start.81 = (f32[384]{0:T(512)}, f32[384]{0:T(512)S(1)}, u32[]{:S(2)}) copy-start(f32[384]{0:T(512)S(1)} %get-tuple-element.94) | copy-start | bytes 4612
  24.7 18.8 %copy-start.83 = (f32[384]{0:T(512)}, f32[384]{0:T(512)S(1)}, u32[]{:S(2)}) copy-start(f32[384]{0:T(512)S(1)} %get-tuple-element.95) | copy-start | bytes 4612
  24.7 5.8 collective-permute-start.3
  45.4 105.1 %copy-start.2 = (bf16[32,32,384]{2,1,0:T(8,128)(2,1)S(1)}, bf16[32,32,384]{2,1,0:T(8,128)(2,1)}, u32[]{:S(2)}) copy-start(bf16[32,32,384]{2,1,0:T(8,128)(2,1)} %param.12) | copy-start | bytes 2359300
  178.2 202.3 %reduce-scatter.5.cloned.1.call-start = ((), (), s32[]{:S(2)}) async-start(), calls=%async_computation.5 | async-start | bytes 2506752 | tf_op jit(solution)/shard_map/reduce_scatter | solution.py:163
  183.4 270.6 %reduce-scatter.3.cloned.1.call-start = ((), (), s32[]{:S(2)}) async-start(), calls=%async_computation.4 | async-start | bytes 2506752 | tf_op jit(solution)/shard_map/reduce_scatter | solution.py:162
  189.3 408.0 %all-reduce.6.cloned.1.call-start = ((), (), s32[]{:S(2)}) async-start(), calls=%async_computation.7 | async-start | bytes 761856 | tf_op jit(solution)/shard_map/psum | solution.py:165
  189.4 6.8 %collective-permute-start.4 = (bf16[32,3,384]{2,1,0:T(4,128)(2,1)S(1)}, bf16[32,3,384]{2,1,0:T(4,128)(2,1)S(1)}, u32[]{:S(2)}, u32[]{:S(2)}) collective-permute-start(bf16[32,3,384]{2,1,0:T(4,128)(2,1)S(1)} %get-tuple-element.117), channel_id=1, source_target_pairs={{0,1},{1,2},{2,3},{3,4},{4,5},{5,6},{6,7},{7,8},{8,9},{9,10},{10,1... | collective-permute-start | bytes 221192 | tf_op jit(solution)/shard_map/ppermute | solution.py:30
  190.1 6.1 %collective-permute-start.5 = (bf16[32,3,384]{2,1,0:T(4,128)(2,1)S(1)}, bf16[32,3,384]{2,1,0:T(4,128)(2,1)S(1)}, u32[]{:S(2)}, u32[]{:S(2)}) collective-permute-start(bf16[32,3,384]{2,1,0:T(4,128)(2,1)S(1)} %get-tuple-element.118), channel_id=1, source_target_pairs={{1,0},{2,1},{3,2},{4,3},{5,4},{6,5},{7,6},{8,7},{9,8},{10,9},{11,1... | collective-permute-start | bytes 221192 | tf_op jit(solution)/shard_map/ppermute | solution.py:31
  196.8 257.2 %copy-start.1 = (bf16[32,32,384]{2,1,0:T(8,128)(2,1)S(1)}, bf16[32,32,384]{2,1,0:T(8,128)(2,1)}, u32[]{:S(2)}) copy-start(bf16[32,32,384]{2,1,0:T(8,128)(2,1)} %param.23) | copy-start | bytes 2359300
  196.8 257.2 %copy-start.8 = (f32[384]{0:T(512)S(1)}, f32[384]{0:T(512)}, u32[]{:S(2)}) copy-start(f32[384]{0:T(512)} %copy-done.7) | copy-start | bytes 4612
  196.8 257.2 %copy-start.10 = (f32[384]{0:T(512)S(1)}, f32[384]{0:T(512)}, u32[]{:S(2)}) copy-start(f32[384]{0:T(512)} %copy-done.9) | copy-start | bytes 4612
  196.8 257.2 %copy-start.12 = (f32[384]{0:T(512)S(1)}, f32[384]{0:T(512)}, u32[]{:S(2)}) copy-start(f32[384]{0:T(512)} %copy-done.11) | copy-start | bytes 4612
  196.9 257.2 %copy-start.14 = (f32[384]{0:T(512)S(1)}, f32[384]{0:T(512)}, u32[]{:S(2)}) copy-start(f32[384]{0:T(512)} %copy-done.13) | copy-start | bytes 4612
  196.9 257.2 %copy-start.16 = (f32[384]{0:T(512)S(1)}, f32[384]{0:T(512)}, u32[]{:S(2)}) copy-start(f32[384]{0:T(512)} %copy-done.15) | copy-start | bytes 4612
  196.9 257.2 %copy-start.18 = (f32[384]{0:T(512)S(1)}, f32[384]{0:T(512)}, u32[]{:S(2)}) copy-start(f32[384]{0:T(512)} %copy-done.17) | copy-start | bytes 4612
  196.9 257.2 %copy-start.20 = (f32[384]{0:T(512)S(1)}, f32[384]{0:T(512)}, u32[]{:S(2)}) copy-start(f32[384]{0:T(512)} %copy-done.19) | copy-start | bytes 4612
  196.9 257.2 %copy-start.22 = (f32[384]{0:T(512)S(1)}, f32[384]{0:T(512)}, u32[]{:S(2)}) copy-start(f32[384]{0:T(512)} %copy-done.21) | copy-start | bytes 4612
  196.9 257.2 %copy-start.24 = (f32[384]{0:T(512)S(1)}, f32[384]{0:T(512)}, u32[]{:S(2)}) copy-start(f32[384]{0:T(512)} %copy-done.23) | copy-start | bytes 4612
  196.9 257.2 %copy-start.26 = (f32[384]{0:T(512)S(1)}, f32[384]{0:T(512)}, u32[]{:S(2)}) copy-start(f32[384]{0:T(512)} %copy-done.25) | copy-start | bytes 4612
  196.9 257.2 %copy-start.28 = (f32[384]{0:T(512)S(1)}, f32[384]{0:T(512)}, u32[]{:S(2)}) copy-start(f32[384]{0:T(512)} %copy-done.27) | copy-start | bytes 4612
  196.9 257.2 %copy-start.30 = (f32[384]{0:T(512)S(1)}, f32[384]{0:T(512)}, u32[]{:S(2)}) copy-start(f32[384]{0:T(512)} %copy-done.29) | copy-start | bytes 4612
  196.9 257.2 %copy-start.32 = (f32[384]{0:T(512)S(1)}, f32[384]{0:T(512)}, u32[]{:S(2)}) copy-start(f32[384]{0:T(512)} %copy-done.31) | copy-start | bytes 4612
  197.0 257.2 %copy-start.34 = (f32[384]{0:T(512)S(1)}, f32[384]{0:T(512)}, u32[]{:S(2)}) copy-start(f32[384]{0:T(512)} %copy-done.33) | copy-start | bytes 4612
  197.0 257.2 %copy-start.36 = (f32[384]{0:T(512)S(1)}, f32[384]{0:T(512)}, u32[]{:S(2)}) copy-start(f32[384]{0:T(512)} %copy-done.35) | copy-start | bytes 4612
  197.0 257.2 %copy-start.38 = (f32[384]{0:T(512)S(1)}, f32[384]{0:T(512)}, u32[]{:S(2)}) copy-start(f32[384]{0:T(512)} %copy-done.37) | copy-start | bytes 4612
  197.0 257.2 %copy-start.40 = (f32[384]{0:T(512)S(1)}, f32[384]{0:T(512)}, u32[]{:S(2)}) copy-start(f32[384]{0:T(512)} %copy-done.39) | copy-start | bytes 4612
  197.0 257.2 %copy-start.42 = (f32[384]{0:T(512)S(1)}, f32[384]{0:T(512)}, u32[]{:S(2)}) copy-start(f32[384]{0:T(512)} %copy-done.41) | copy-start | bytes 4612
  197.0 257.2 %copy-start.44 = (f32[384]{0:T(512)S(1)}, f32[384]{0:T(512)}, u32[]{:S(2)}) copy-start(f32[384]{0:T(512)} %copy-done.43) | copy-start | bytes 4612
  197.0 257.2 %copy-start.46 = (f32[384]{0:T(512)S(1)}, f32[384]{0:T(512)}, u32[]{:S(2)}) copy-start(f32[384]{0:T(512)} %copy-done.45) | copy-start | bytes 4612
  197.0 257.2 %copy-start.48 = (f32[384]{0:T(512)S(1)}, f32[384]{0:T(512)}, u32[]{:S(2)}) copy-start(f32[384]{0:T(512)} %copy-done.47) | copy-start | bytes 4612
  197.0 257.2 %copy-start.50 = (f32[384]{0:T(512)S(1)}, f32[384]{0:T(512)}, u32[]{:S(2)}) copy-start(f32[384]{0:T(512)} %copy-done.49) | copy-start | bytes 4612
  197.0 257.2 %copy-start.52 = (f32[384]{0:T(512)S(1)}, f32[384]{0:T(512)}, u32[]{:S(2)}) copy-start(f32[384]{0:T(512)} %copy-done.51) | copy-start | bytes 4612
  197.1 257.2 %copy-start.54 = (f32[384]{0:T(512)S(1)}, f32[384]{0:T(512)}, u32[]{:S(2)}) copy-start(f32[384]{0:T(512)} %copy-done.53) | copy-start | bytes 4612
  197.1 257.2 %copy-start.56 = (f32[384]{0:T(512)S(1)}, f32[384]{0:T(512)}, u32[]{:S(2)}) copy-start(f32[384]{0:T(512)} %copy-done.55) | copy-start | bytes 4612
  197.1 257.2 %copy-start.58 = (f32[384]{0:T(512)S(1)}, f32[384]{0:T(512)}, u32[]{:S(2)}) copy-start(f32[384]{0:T(512)} %copy-done.57) | copy-start | bytes 4612
  197.1 257.2 %copy-start.60 = (f32[384]{0:T(512)S(1)}, f32[384]{0:T(512)}, u32[]{:S(2)}) copy-start(f32[384]{0:T(512)} %copy-done.59) | copy-start | bytes 4612
  197.1 257.2 %copy-start.62 = (f32[384]{0:T(512)S(1)}, f32[384]{0:T(512)}, u32[]{:S(2)}) copy-start(f32[384]{0:T(512)} %copy-done.61) | copy-start | bytes 4612
  197.1 257.2 %copy-start.64 = (f32[384]{0:T(512)S(1)}, f32[384]{0:T(512)}, u32[]{:S(2)}) copy-start(f32[384]{0:T(512)} %copy-done.63) | copy-start | bytes 4612
  197.1 257.2 %copy-start.66 = (f32[384]{0:T(512)S(1)}, f32[384]{0:T(512)}, u32[]{:S(2)}) copy-start(f32[384]{0:T(512)} %copy-done.65) | copy-start | bytes 4612
  197.1 257.2 %copy-start.68 = (f32[384]{0:T(512)S(1)}, f32[384]{0:T(512)}, u32[]{:S(2)}) copy-start(f32[384]{0:T(512)} %copy-done.67) | copy-start | bytes 4612
  197.1 257.2 %copy-start.70 = (f32[384]{0:T(512)S(1)}, f32[384]{0:T(512)}, u32[]{:S(2)}) copy-start(f32[384]{0:T(512)} %copy-done.69) | copy-start | bytes 4612
  197.1 257.2 %copy-start.72 = (f32[384]{0:T(512)S(1)}, f32[384]{0:T(512)}, u32[]{:S(2)}) copy-start(f32[384]{0:T(512)} %copy-done.71) | copy-start | bytes 4612
  197.2 257.2 %copy-start.74 = (f32[384]{0:T(512)S(1)}, f32[384]{0:T(512)}, u32[]{:S(2)}) copy-start(f32[384]{0:T(512)} %copy-done.73) | copy-start | bytes 4612
  197.2 257.2 %copy-start.76 = (f32[384]{0:T(512)S(1)}, f32[384]{0:T(512)}, u32[]{:S(2)}) copy-start(f32[384]{0:T(512)} %copy-done.75) | copy-start | bytes 4612
  197.2 257.2 %copy-start.78 = (f32[384]{0:T(512)S(1)}, f32[384]{0:T(512)}, u32[]{:S(2)}) copy-start(f32[384]{0:T(512)} %copy-done.77) | copy-start | bytes 4612
  197.2 257.2 %copy-start.80 = (f32[384]{0:T(512)S(1)}, f32[384]{0:T(512)}, u32[]{:S(2)}) copy-start(f32[384]{0:T(512)} %copy-done.79) | copy-start | bytes 4612
  197.2 257.2 %copy-start.82 = (f32[384]{0:T(512)S(1)}, f32[384]{0:T(512)}, u32[]{:S(2)}) copy-start(f32[384]{0:T(512)} %copy-done.81) | copy-start | bytes 4612
  197.2 257.2 %copy-start.84 = (f32[384]{0:T(512)S(1)}, f32[384]{0:T(512)}, u32[]{:S(2)}) copy-start(f32[384]{0:T(512)} %copy-done.83) | copy-start | bytes 4612
  197.2 2.6 collective-permute-start.6
  198.5 5.7 collective-permute-start.7
  (46 other events, 333.8 us)
Sparse Core Ops, SparseCore 0:
  9.8 71.6 all-gather.2
  83.3 67.1 all-gather.4
  178.3 125.8 all-reduce.3
  306.8 73.6 reduce-scatter.4
  383.0 70.9 reduce-scatter.2
  456.9 140.2 all-reduce.5
